TPU v7x, 32 devices: a whole 2x2x4 slice. The times are simulated.
32 devices in a mesh: groups: 2 (over x), corpus: 16 (over z, y, core).
Axes of the slice: x: 2, y: 2, z: 4, core: 2. Of those that a mesh axis runs over, the one named last changes fastest.
Arguments:
- queries: bfloat16 [1792, 32, 128], P(('groups', 'corpus')), parts along dimension 0, may hold values from -6 to 6
- passages: bfloat16 [4096, 128, 128], P(('groups', 'corpus')), parts along dimension 0, may hold values from -0.5 to 0.5
- lengths: int32 [4096], P(('groups', 'corpus')), parts along dimension 0, may hold values from 8 to 128
- candidates: int32 [32, 128], P(('groups', 'corpus')), parts along dimension 0, may hold values from 0 to 2047, as said below
Outputs:
- scores: float32 [1792, 128], P(('groups', 'corpus')), parts along dimension 0
- best_scores: float32 [1792, 100], P(('groups', 'corpus')), parts along dimension 0
There are 2 independent parts, one for each index of `groups`. A program takes and returns all parts, laid end to end along the dimension named above; each array names one. Nothing has to cross between parts.
Inputs may be any that keep to these rules, and one draw needn't show every extreme that they name: Row b lists the candidates of queries b * 56 to (b + 1) * 56 - 1. Passage p is held by owner p // 128. In every row at most 12 entries share an owner, and in every row some owner holds exactly 12 of them. Entries may repeat. `lengths`: rows of a tile at or past its length are padding.
All inputs are finite; a program needn't handle non-finite values.
Results may differ from a plain program's by a relative error of at most 0.0003.
Values may be sent and summed in bfloat16 or wider, within the bound.
A program may use at most 128 MiB of HBM per device.

v0:
```python
import math
import jax
import jax.numpy as jnp
from jax import lax
from jax.sharding import PartitionSpec as P

TOPK = 100


def maxsim_many(query_sets, tile_sets, per_device):
    similar = jnp.einsum(
        "srd,sgpd->srgp", query_sets, tile_sets, preferred_element_type=jnp.float32
    )
    nearest = jnp.max(similar, axis=3)
    shards_now = query_sets.shape[0]
    query_tok = query_sets.shape[1] // per_device
    return jnp.sum(
        nearest.reshape(shards_now, per_device, query_tok, nearest.shape[2]), axis=2
    ) / float(query_tok)


def fill_rows(tile_set, tile_len):
    inside = lax.broadcasted_iota(jnp.int32, tile_set.shape[:2], 1) < tile_len[:, None]
    return jnp.where(inside[:, :, None], tile_set, tile_set[:, :1, :])


def local(queries, passages, lengths, candidates):
    peers = lax.axis_size("corpus")
    per_owner, tile_rows, feature = passages.shape
    per_device, query_tok = (queries.shape[0], queries.shape[1])
    candidate_ids = candidates[0]
    number = candidate_ids.shape[0]
    capacity = max(2, 3 * number // (2 * peers))
    owner_of = candidate_ids // per_owner
    local_id = candidate_ids - owner_of * per_owner
    position = jnp.arange(number, dtype=jnp.int32)
    shared = (owner_of[:, None] == owner_of[None, :]) & (position[None, :] < position[:, None])
    rank_in = jnp.sum(shared.astype(jnp.int32), axis=1)
    slot_of = owner_of * capacity + rank_in
    matches = slot_of[None, :] == jnp.arange(peers * capacity, dtype=jnp.int32)[:, None]
    wanted = jnp.max(jnp.where(matches, local_id[None, :], -1), axis=1).reshape(peers, capacity)
    asked = lax.all_to_all(wanted, "corpus", split_axis=0, concat_axis=0, tiled=True)
    picked = jnp.maximum(asked.reshape(-1), 0)
    chosen = fill_rows(passages[picked], lengths[picked])
    by_scorer = chosen.reshape(peers, capacity, tile_rows, feature)
    stacked = queries.reshape(1, per_device * query_tok, feature)
    piece = lax.all_gather(stacked, "corpus", axis=0, tiled=True)
    shards_here = piece.shape[0]
    group_size = math.gcd(shards_here, 8)
    turns = shards_here // group_size
    query_groups = piece.reshape(turns, group_size, piece.shape[1], feature)
    tile_groups = by_scorer.reshape(turns, group_size, capacity, tile_rows, feature)
    fresh_scores = lax.map(
        lambda paired: maxsim_many(paired[0], paired[1], per_device), (query_groups, tile_groups)
    )
    fresh_scores = fresh_scores.reshape(shards_here, per_device, capacity)
    returned = lax.all_to_all(fresh_scores, "corpus", split_axis=0, concat_axis=0, tiled=True)
    spread = jnp.transpose(returned, (1, 0, 2)).reshape(per_device, peers * capacity)
    scores = jnp.take(spread, slot_of, axis=1)
    best_scores = lax.top_k(scores, TOPK)[0]
    return (scores, best_scores)


def solution(mesh):
    return jax.shard_map(
        local,
        mesh=mesh,
        in_specs=(
            P(("groups", "corpus"), None, None),
            P(("groups", "corpus"), None, None),
            P(("groups", "corpus")),
            P(("groups", "corpus"), None),
        ),
        out_specs=(P(("groups", "corpus"), None), P(("groups", "corpus"), None)),
        check_vma=False,
    )
```

profile of v0, /device:TPU:0, one launch (start us, length us, event | category | flops | bytes accessed | tf_op | source)
XLA Modules:
  0.0 137.0 jit_solution(5977993929277204286)
XLA Ops:
  7.2 0.0 copy-start
  7.2 0.0 all-gather.2.cloned.1.call-start
  7.2 0.7 all-gather.2.cloned.1.call-update
  7.9 0.7 subtract_bitcast_fusion
  8.6 0.7 and_select_fusion.2
  9.2 0.2 convert_reduce_fusion
  9.4 0.1 select_reduce_fusion
  9.6 0.7 all_to_all.9
  10.3 7.4 %all-to-all-start = ((s32[16,1,12]{2,1,0:T(1,128)}), s32[16,1,12]{2,1,0:T(1,128)S(1)}, u32[]{:S(2)}, u32[]{:S(2)}) async-start(s32[16,1,12]{2,1,0:T(1,128)} %bitcast.12), calls=%async_computation | async-start | bytes 16384 | tf_op jit(solution)/shard_map/all_to_all | solution.py:42
  17.7 0.7 fusion.6
  18.3 0.7 compare_and_fusion
  19.0 5.0 %all-to-all-done = s32[16,1,12]{2,1,0:T(1,128)S(1)} async-done(((s32[16,1,12]{2,1,0:T(1,128)}), s32[16,1,12]{2,1,0:T(1,128)S(1)}, u32[]{:S(2)}, u32[]{:S(2)}) %all-to-all-start) | async-done | bytes 800 | tf_op jit(solution)/shard_map/all_to_all | solution.py:42
  24.1 0.1 reshape.184
  24.2 10.2 %gather_fusion.1 = bf16[192,128,128]{2,1,0:T(8,128)(2,1)} fusion(bf16[128,128,128]{2,1,0:T(8,128)(2,1)} %param.7, s32[1024]{0:T(1024)S(1)} %pad_clamp_fusion.1), kind=kCustom, calls=%fused_computation.1 | custom fusion | bytes 12583680 | tf_op jit(solution)/shard_map/gather | solution.py:44
  34.3 1.3 slice_reduce_fusion
  35.6 0.0 copy-done
  35.6 1.6 %gather_fusion = s32[192]{0:T(256)S(1)} fusion(s32[128]{0:T(128)S(1)} %copy-done, s32[1024]{0:T(1024)S(1)} %pad_clamp_fusion.1), kind=kCustom, calls=%fused_computation | custom fusion | bytes 2304 | tf_op jit(solution)/shard_map/gather | solution.py:44
  37.2 0.1 lt.53
  37.3 0.1 iota_compare_fusion
  37.4 6.5 %broadcast_select_fusion = bf16[2,8,12,128,128]{4,3,2,1,0:T(8,128)(2,1)} fusion(bf16[2,8,12,128,128]{4,3,2,1,0:T(8,128)(2,1)} %bitcast.73, pred[2,8,12,128]{3,2,1,0:T(8,128)(4,1)S(1)} %iota_compare_fusion, bf16[2,8,12,128]{3,2,1,0:T(8,128)(2,1)S(1)} %broadcast_in_dim.64), kind=kLoop, calls=%fused_computation.10 | loop fusion | flops 3145728 | bytes 12656640 | tf_op jit(solution)/shard_map/jit(_where)/select_n | solution.py:24
  43.9 36.8 %all-gather.2.cloned.1.call-done = bf16[16,1792,128]{2,1,0:T(8,128)(2,1)} async-done(((bf16[1,1792,128]{2,1,0:T(8,128)(2,1)}), bf16[16,1792,128]{2,1,0:T(8,128)(2,1)}) %all-gather.2.cloned.1.call-update) | async-done | bytes 7340048 | tf_op jit(solution)/shard_map/all_gather | solution.py:47
  80.7 32.9 %while.10 = (s32[]{:T(128)}, f32[2,8,56,12]{2,1,0,3:T(8,128)S(1)}, bf16[2,8,1792,128]{3,2,1,0:T(8,128)(2,1)}, bf16[2,8,12,128,128]{4,3,2,1,0:T(8,128)(2,1)}, s32[]{:T(128)}, /*index=5*/f32[]{:T(128)}) while((s32[]{:T(128)}, f32[2,8,56,12]{2,1,0,3:T(8,128)S(1)}, bf16[2,8,1792,128]{3,2,1,0:T(8,128)(2,1)}, ...), condition=%wide.region_5.6_spmd, body=%wide.region_2.5_spmd.sunk | while | flops 5659164672 | bytes 11065421 | solution.py:53
  80.7 14.4 %convolution_reduce_fusion.2 = f32[8,1792,12]{1,2,0:T(8,128)S(1)} fusion(bf16[2,8,1792,128]{3,2,1,0:T(8,128)(2,1)} %get-tuple-element.87, s32[]{:T(128)} %get-tuple-element.79, bf16[2,8,12,128,128]{4,3,2,1,0:T(8,128)(2,1)} %get-tuple-element.88), kind=kOutput, calls=%fused_computation.3.clone.1 | convolution fusion | flops 5658992640 | bytes 7504896 | tf_op jit(solution)/shard_map/while/body/eval_jaxpr/srd,sgpd->srgp/dot_general | solution.py:11
  95.1 0.4 copy.35
  95.5 0.8 reshape.220
  96.4 0.8 reduce_sum.27
  97.2 14.4 %convolution_reduce_fusion.2 = f32[8,1792,12]{1,2,0:T(8,128)S(1)} fusion(bf16[2,8,1792,128]{3,2,1,0:T(8,128)(2,1)} %get-tuple-element.87, s32[]{:T(128)} %get-tuple-element.79, bf16[2,8,12,128,128]{4,3,2,1,0:T(8,128)(2,1)} %get-tuple-element.88), kind=kOutput, calls=%fused_computation.3.clone.1 | convolution fusion | flops 5658992640 | bytes 7504896 | tf_op jit(solution)/shard_map/while/body/eval_jaxpr/srd,sgpd->srgp/dot_general | solution.py:11
  111.6 0.4 copy.35
  112.0 0.8 reshape.220
  112.8 0.8 reduce_sum.27
  113.7 0.8 reshape.217
  114.5 3.5 %all-to-all-start.1 = ((f32[16,1,672]{2,1,0:T(1,128)}), f32[16,1,672]{2,1,0:T(1,128)S(1)}, u32[]{:S(2)}, u32[]{:S(2)}) async-start(f32[16,1,672]{2,1,0:T(1,128)} %reshape.217), calls=%async_computation.1 | async-start | bytes 98304 | tf_op jit(solution)/shard_map/all_to_all | solution.py:57
  118.0 6.7 %all-to-all-done.1 = f32[16,1,672]{2,1,0:T(1,128)S(1)} async-done(((f32[16,1,672]{2,1,0:T(1,128)}), f32[16,1,672]{2,1,0:T(1,128)S(1)}, u32[]{:S(2)}, u32[]{:S(2)}) %all-to-all-start.1) | async-done | bytes 43040 | tf_op jit(solution)/shard_map/all_to_all | solution.py:57
  124.7 0.5 broadcast.219
  125.2 0.8 reduce.6
  126.0 0.1 reshape.218
  126.1 0.6 gather_fusion.2
  126.8 0.1 select_bitcast_fusion
  126.9 0.1 copy.27
  126.9 0.0 copy-start.1
  126.9 3.2 %top_k.9 = (f32[56,128]{1,0:T(8,128)}, s32[56,128]{1,0:T(8,128)}) sort(f32[56,128]{1,0:T(8,128)S(1)} %copy.27, s32[56,128]{1,0:T(8,128)S(1)} %iota.22), dimensions={1}, to_apply=%region_6.7 | sort | flops 93184 | bytes 114688 | tf_op jit(solution)/shard_map/top_k | solution.py:60
  130.1 0.0 copy-done.1
  (12 shorter events, 0.1 us)
Async XLA Ops:
  7.2 28.5 %copy-start = (s32[128]{0:T(128)S(1)}, s32[128]{0:T(128)}, u32[]{:S(2)}) copy-start(s32[128]{0:T(128)} %param.8) | copy-start | bytes 1540
  7.2 73.5 %all-gather.2.cloned.1.call-start = ((), (), s32[]{:S(2)}) async-start(), calls=%async_computation.2 | async-start | bytes 7798784 | tf_op jit(solution)/shard_map/all_gather | solution.py:47
  10.3 13.8 %all-to-all-start = ((s32[16,1,12]{2,1,0:T(1,128)}), s32[16,1,12]{2,1,0:T(1,128)S(1)}, u32[]{:S(2)}, u32[]{:S(2)}) async-start(s32[16,1,12]{2,1,0:T(1,128)} %bitcast.12), calls=%async_computation | async-start | bytes 16384 | tf_op jit(solution)/shard_map/all_to_all | solution.py:42
  114.5 10.2 %all-to-all-start.1 = ((f32[16,1,672]{2,1,0:T(1,128)}), f32[16,1,672]{2,1,0:T(1,128)S(1)}, u32[]{:S(2)}, u32[]{:S(2)}) async-start(f32[16,1,672]{2,1,0:T(1,128)} %reshape.217), calls=%async_computation.1 | async-start | bytes 98304 | tf_op jit(solution)/shard_map/all_to_all | solution.py:57
  126.9 3.2 %copy-start.1 = (f32[56,128]{1,0:T(8,128)}, f32[56,128]{1,0:T(8,128)S(1)}, u32[]{:S(2)}) copy-start(f32[56,128]{1,0:T(8,128)S(1)} %copy.27) | copy-start | bytes 86020
Sparse Core Ops, SparseCore 0:
  10.3 70.3 all-gather.1
where the time goes:
time: 137 us
  waiting for transfers between devices  49.2 us (36%)
  matrix products  28.8 us (21%)
  local copies, waits for them, and re-layouts  18.4 us (13%)
  other arithmetic  15.3 us (11%)
  between operations  14.2 us (10%)
  starting transfers between devices  10.9 us (8%)
    all_gather x1, waiting for transfers between devices, local(): piece = lax.all_gather(stacked, 'corpus', axis=0, tiled=True)  36.8 us
    dot_general x2, matrix products, maxsim_many(): jnp.einsum('srd,sgpd->srgp', query_sets, tile_sets, preferred_element_typ...  28.8 us
    gather x2, local copies, waits for them, and re-layouts, local(): chosen = fill_rows(passages[picked], lengths[picked])  11.7 us
    all_to_all x1, starting transfers between devices, local(): lax.all_to_all(wanted, 'corpus', split_axis=0, concat_axis=0, tiled=True)  7.41 us
    all_to_all x1, waiting for transfers between devices, local(): lax.all_to_all(fresh_scores, 'corpus', split_axis=0, concat_axis=0, tiled...  6.72 us
    select_n x1, other arithmetic, fill_rows(): return jnp.where(inside[:, :, None], tile_set, tile_set[:, :1, :])  6.55 us
    all_to_all x1, waiting for transfers between devices, local(): lax.all_to_all(wanted, 'corpus', split_axis=0, concat_axis=0, tiled=True)  5.01 us
    all_to_all x1, starting transfers between devices, local(): lax.all_to_all(fresh_scores, 'corpus', split_axis=0, concat_axis=0, tiled...  3.5 us
  transfers between devices with their start and end apart: 3, of which 3 were waited for; matrix products, arithmetic and copies ran while one was open for 17% of the time, Pallas kernels for 0%

commit v1 on v0

--- a/solution.py
+++ b/solution.py
@@ -5,6 +5,19 @@
 from jax.sharding import PartitionSpec as P
 
 TOPK = 100
+
+
+def gather_around(array, axis, dim):
+    ways = lax.axis_size(axis)
+    up = [(d, (d + 1) % ways) for d in range(ways)]
+    down = [(d, (d - 1) % ways) for d in range(ways)]
+    earlier, later = ([array], [array])
+    for _ in range(ways // 2):
+        earlier.append(lax.ppermute(earlier[-1], axis, up))
+    for _ in range((ways - 1) // 2):
+        later.append(lax.ppermute(later[-1], axis, down))
+    line = jnp.concatenate([*earlier[::-1], *later[1:]], axis=dim)
+    return jnp.roll(line, (lax.axis_index(axis) - ways // 2) * array.shape[dim], axis=dim)
 
 
 def maxsim_many(query_sets, tile_sets, per_device):
@@ -44,7 +57,7 @@
     chosen = fill_rows(passages[picked], lengths[picked])
     by_scorer = chosen.reshape(peers, capacity, tile_rows, feature)
     stacked = queries.reshape(1, per_device * query_tok, feature)
-    piece = lax.all_gather(stacked, "corpus", axis=0, tiled=True)
+    piece = gather_around(stacked, "corpus", 0)
     shards_here = piece.shape[0]
     group_size = math.gcd(shards_here, 8)
     turns = shards_here // group_size

time: 137 us -> 194 us (1.42)
  local copies, waits for them, and re-layouts: 18.4 us -> 59.3 us
  starting transfers between devices: 10.9 us -> 42.9 us
  between operations: 14.2 us -> 0.92 us
  waiting for transfers between devices: 49.2 us -> 46.8 us
    all_gather x1 -> x0, waiting for transfers between devices: 36.8 us -> none  [local(): piece = lax.all_gather(stacked, 'corpus', axis=0, tiled=True)]
    ppermute x0 -> x15, waiting for transfers between devices: none -> 34.5 us  [the longest x8 34.4 us: gather_around(): earlier.append(lax.ppermute(earlier[-1], axis, up))]
    unnamed x7 -> x50, local copies, waits for them, and re-layouts: 0.95 us -> 34.2 us
    ppermute x0 -> x15, starting transfers between devices: none -> 32.5 us  [the longest x7 23.6 us: gather_around(): later.append(lax.ppermute(later[-1], axis, down))]
    dynamic_slice x0 -> x1, local copies, waits for them, and re-layouts: none -> 6.73 us  [gather_around(): jnp.roll(line, (lax.axis_index(axis) - ways // 2) * array.shape[dim], axi...]
  transfers between devices with their start and end apart: 3 -> 17, of which waited for: 3 -> 7; matrix products, arithmetic and copies ran while one was open for 17% -> 20% of each run, Pallas kernels for 0% -> 0%
where the time goes in v1:
time: 194 us; the launch traced here: 193 us
  local copies, waits for them, and re-layouts  59.3 us (31%)
  waiting for transfers between devices  46.8 us (24%)
  starting transfers between devices  42.9 us (22%)
  matrix products  28.8 us (15%)
  other arithmetic  14.6 us (8%)
    ppermute x8, waiting for transfers between devices, gather_around(): earlier.append(lax.ppermute(earlier[-1], axis, up))  34.4 us
    unnamed x50, local copies, waits for them, and re-layouts  34.2 us
    dot_general x2, matrix products, maxsim_many(): jnp.einsum('srd,sgpd->srgp', query_sets, tile_sets, preferred_element_typ...  28.8 us
    ppermute x7, starting transfers between devices, gather_around(): later.append(lax.ppermute(later[-1], axis, down))  23.6 us
    gather x2, local copies, waits for them, and re-layouts, local(): chosen = fill_rows(passages[picked], lengths[picked])  11.8 us
    ppermute x8, starting transfers between devices, gather_around(): earlier.append(lax.ppermute(earlier[-1], axis, up))  8.96 us
    all_to_all x1, starting transfers between devices, local(): lax.all_to_all(wanted, 'corpus', split_axis=0, concat_axis=0, tiled=True)  6.83 us
    dynamic_slice x1, local copies, waits for them, and re-layouts, gather_around(): jnp.roll(line, (lax.axis_index(axis) - ways // 2) * array.shape[dim], axi...  6.73 us
  transfers between devices with their start and end apart: 17, of which 7 were waited for; matrix products, arithmetic and copies ran while one was open for 20% of the time, Pallas kernels for 0%

profile of v1, /device:TPU:0, one launch (start us, length us, event | category | flops | bytes accessed | tf_op | source)
XLA Modules:
  0.0 193.4 jit_solution(15736280296141465445)
XLA Ops:
  1.2 11.4 %collective-permute-done = bf16[1,1792,128]{2,1,0:T(8,128)(2,1)S(1)} collective-permute-done((bf16[1,1792,128]{2,1,0:T(8,128)(2,1)}, bf16[1,1792,128]{2,1,0:T(8,128)(2,1)S(1)}, u32[]{:S(2)}, u32[]{:S(2)}) %collective-permute-start) | collective-permute-done | bytes 458784 | tf_op jit(solution)/shard_map/ppermute | solution.py:16
  12.6 4.4 %collective-permute-start.8 = (bf16[1,1792,128]{2,1,0:T(8,128)(2,1)}, bf16[1,1792,128]{2,1,0:T(8,128)(2,1)S(1)}, u32[]{:S(2)}, u32[]{:S(2)}) collective-permute-start(bf16[1,1792,128]{2,1,0:T(8,128)(2,1)} %bitcast.80), channel_id=1, source_target_pairs={{0,15},{1,0},{2,1},{3,2},{4,3},{5,4},{6,5},{7,6},{8,7},{9,8},{10,9... | collective-permute-start | bytes 1376264 | tf_op jit(solution)/shard_map/ppermute | solution.py:18
  17.0 6.3 %collective-permute-done.1 = bf16[1,1792,128]{2,1,0:T(8,128)(2,1)S(1)} collective-permute-done((bf16[1,1792,128]{2,1,0:T(8,128)(2,1)S(1)}, bf16[1,1792,128]{2,1,0:T(8,128)(2,1)S(1)}, u32[]{:S(2)}, u32[]{:S(2)}) %collective-permute-start.1) | collective-permute-done | bytes 458784 | tf_op jit(solution)/shard_map/ppermute | solution.py:16
  23.3 4.6 %collective-permute-start.9 = (bf16[1,1792,128]{2,1,0:T(8,128)(2,1)S(1)}, bf16[1,1792,128]{2,1,0:T(8,128)(2,1)S(1)}, u32[]{:S(2)}, u32[]{:S(2)}) collective-permute-start(bf16[1,1792,128]{2,1,0:T(8,128)(2,1)S(1)} %collective-permute-done.8), channel_id=1, source_target_pairs={{0,15},{1,0},{2,1},{3,2},{4,3},{5,4},{6,5},{7,6},{8,7},{9,8},{10,9... | collective-permute-start | bytes 1376264 | tf_op jit(solution)/shard_map/ppermute | solution.py:18
  27.9 6.1 %collective-permute-done.2 = bf16[1,1792,128]{2,1,0:T(8,128)(2,1)S(1)} collective-permute-done((bf16[1,1792,128]{2,1,0:T(8,128)(2,1)S(1)}, bf16[1,1792,128]{2,1,0:T(8,128)(2,1)S(1)}, u32[]{:S(2)}, u32[]{:S(2)}) %collective-permute-start.2) | collective-permute-done | bytes 458784 | tf_op jit(solution)/shard_map/ppermute | solution.py:16
  34.0 1.0 collective-permute-start.3
  35.0 3.6 %collective-permute-start.10 = (bf16[1,1792,128]{2,1,0:T(8,128)(2,1)S(1)}, bf16[1,1792,128]{2,1,0:T(8,128)(2,1)S(1)}, u32[]{:S(2)}, u32[]{:S(2)}) collective-permute-start(bf16[1,1792,128]{2,1,0:T(8,128)(2,1)S(1)} %collective-permute-done.9), channel_id=1, source_target_pairs={{0,15},{1,0},{2,1},{3,2},{4,3},{5,4},{6,5},{7,6},{8,7},{9,8},{10,9... | collective-permute-start | bytes 1376264 | tf_op jit(solution)/shard_map/ppermute | solution.py:18
  38.6 6.1 %collective-permute-done.3 = bf16[1,1792,128]{2,1,0:T(8,128)(2,1)S(1)} collective-permute-done((bf16[1,1792,128]{2,1,0:T(8,128)(2,1)S(1)}, bf16[1,1792,128]{2,1,0:T(8,128)(2,1)S(1)}, u32[]{:S(2)}, u32[]{:S(2)}) %collective-permute-start.3) | collective-permute-done | bytes 458784 | tf_op jit(solution)/shard_map/ppermute | solution.py:16
  44.7 2.4 %collective-permute-start.4 = (bf16[1,1792,128]{2,1,0:T(8,128)(2,1)S(1)}, bf16[1,1792,128]{2,1,0:T(8,128)(2,1)S(1)}, u32[]{:S(2)}, u32[]{:S(2)}) collective-permute-start(bf16[1,1792,128]{2,1,0:T(8,128)(2,1)S(1)} %collective-permute-done.3), channel_id=1, source_target_pairs={{0,1},{1,2},{2,3},{3,4},{4,5},{5,6},{6,7},{7,8},{8,9},{9,10},{10,1... | collective-permute-start | bytes 1376264 | tf_op jit(solution)/shard_map/ppermute | solution.py:16
  48.6 2.1 %collective-permute-start.11 = (bf16[1,1792,128]{2,1,0:T(8,128)(2,1)S(1)}, bf16[1,1792,128]{2,1,0:T(8,128)(2,1)}, u32[]{:S(2)}, u32[]{:S(2)}) collective-permute-start(bf16[1,1792,128]{2,1,0:T(8,128)(2,1)S(1)} %collective-permute-done.10), channel_id=1, source_target_pairs={{0,15},{1,0},{2,1},{3,2},{4,3},{5,4},{6,5},{7,6},{8,7},{9,8},{10,9... | collective-permute-start | bytes 1376264 | tf_op jit(solution)/shard_map/ppermute | solution.py:18
  50.7 4.7 %collective-permute-done.4 = bf16[1,1792,128]{2,1,0:T(8,128)(2,1)S(1)} collective-permute-done((bf16[1,1792,128]{2,1,0:T(8,128)(2,1)S(1)}, bf16[1,1792,128]{2,1,0:T(8,128)(2,1)S(1)}, u32[]{:S(2)}, u32[]{:S(2)}) %collective-permute-start.4) | collective-permute-done | bytes 458784 | tf_op jit(solution)/shard_map/ppermute | solution.py:16
  55.4 4.5 %collective-permute-start.5 = (bf16[1,1792,128]{2,1,0:T(8,128)(2,1)S(1)}, bf16[1,1792,128]{2,1,0:T(8,128)(2,1)}, u32[]{:S(2)}, u32[]{:S(2)}) collective-permute-start(bf16[1,1792,128]{2,1,0:T(8,128)(2,1)S(1)} %collective-permute-done.4), channel_id=1, source_target_pairs={{0,1},{1,2},{2,3},{3,4},{4,5},{5,6},{6,7},{7,8},{8,9},{9,10},{10,1... | collective-permute-start | bytes 1376264 | tf_op jit(solution)/shard_map/ppermute | solution.py:16
  60.7 6.8 %all-to-all-start = ((s32[16,1,12]{2,1,0:T(1,128)}), s32[16,1,12]{2,1,0:T(1,128)S(1)}, u32[]{:S(2)}, u32[]{:S(2)}) async-start(s32[16,1,12]{2,1,0:T(1,128)} %bitcast.12), calls=%async_computation | async-start | bytes 16384 | tf_op jit(solution)/shard_map/all_to_all | solution.py:55
  68.2 5.7 %all-to-all-done = s32[16,1,12]{2,1,0:T(1,128)S(1)} async-done(((s32[16,1,12]{2,1,0:T(1,128)}), s32[16,1,12]{2,1,0:T(1,128)S(1)}, u32[]{:S(2)}, u32[]{:S(2)}) %all-to-all-start) | async-done | bytes 800 | tf_op jit(solution)/shard_map/all_to_all | solution.py:55
  74.6 10.3 %gather_fusion.1 = bf16[192,128,128]{2,1,0:T(8,128)(2,1)} fusion(bf16[128,128,128]{2,1,0:T(8,128)(2,1)} %param.7, s32[1024]{0:T(1024)S(1)} %get-tuple-element.49), kind=kCustom, calls=%fused_computation.1 | custom fusion | bytes 12583680 | tf_op jit(solution)/shard_map/gather | solution.py:57
  84.9 1.3 slice_reduce_fusion
  86.1 1.6 gather_fusion
  87.9 4.1 %collective-permute-start.13 = (bf16[1,1792,128]{2,1,0:T(8,128)(2,1)}, bf16[1,1792,128]{2,1,0:T(8,128)(2,1)S(1)}, u32[]{:S(2)}, u32[]{:S(2)}) collective-permute-start(bf16[1,1792,128]{2,1,0:T(8,128)(2,1)} %collective-permute-done.12), channel_id=1, source_target_pairs={{0,15},{1,0},{2,1},{3,2},{4,3},{5,4},{6,5},{7,6},{8,7},{9,8},{10,9... | collective-permute-start | bytes 1376264 | tf_op jit(solution)/shard_map/ppermute | solution.py:18
  92.0 6.5 %broadcast_select_fusion = bf16[2,8,12,128,128]{4,3,2,1,0:T(8,128)(2,1)} fusion(bf16[2,8,12,128,128]{4,3,2,1,0:T(8,128)(2,1)} %bitcast.77, pred[2,8,12,128]{3,2,1,0:T(8,128)(4,1)S(1)} %iota_compare_fusion, bf16[2,8,12,128]{3,2,1,0:T(8,128)(2,1)S(1)} %broadcast_in_dim.64), kind=kLoop, calls=%fused_computation.10 | loop fusion | flops 3145728 | bytes 12656640 | tf_op jit(solution)/shard_map/jit(_where)/select_n | solution.py:37
  98.5 4.7 %collective-permute-start.14 = (bf16[1,1792,128]{2,1,0:T(8,128)(2,1)S(1)}, bf16[1,1792,128]{2,1,0:T(8,128)(2,1)S(1)}, u32[]{:S(2)}, u32[]{:S(2)}) collective-permute-start(bf16[1,1792,128]{2,1,0:T(8,128)(2,1)S(1)} %collective-permute-done.13), channel_id=1, source_target_pairs={{0,15},{1,0},{2,1},{3,2},{4,3},{5,4},{6,5},{7,6},{8,7},{9,8},{10,9... | collective-permute-start | bytes 1376264 | tf_op jit(solution)/shard_map/ppermute | solution.py:18
  104.0 1.8 constant_dynamic-update-slice_fusion.30
  105.8 1.8 constant_dynamic-update-slice_fusion.29
  107.7 0.8 constant_dynamic-update-slice_fusion.28
  108.5 0.8 constant_dynamic-update-slice_fusion.27
  110.1 0.8 constant_dynamic-update-slice_fusion.25
  111.7 0.8 constant_dynamic-update-slice_fusion.23
  114.1 0.8 constant_dynamic-update-slice_fusion.20
  115.0 1.9 constant_dynamic-update-slice_fusion.19
  116.8 1.8 constant_dynamic-update-slice_fusion.18
  118.6 0.8 constant_dynamic-update-slice_fusion.17
  119.4 0.8 constant_dynamic-update-slice_fusion.16
  121.0 1.8 constant_dynamic-update-slice_fusion.14
  122.9 1.9 constant_dynamic-update-slice_fusion.13
  124.7 0.8 constant_dynamic-update-slice_fusion.12
  125.6 0.8 constant_dynamic-update-slice_fusion.11
  128.0 0.8 constant_dynamic-update-slice_fusion.8
  128.8 0.8 constant_dynamic-update-slice_fusion.7
  132.0 1.8 constant_dynamic-update-slice_fusion.3
  133.9 1.8 constant_dynamic-update-slice_fusion.2
  137.3 6.7 %constant_dynamic-slice_fusion = bf16[16,1792,128]{2,1,0:T(8,128)(2,1)} fusion(bf16[32,1792,128]{2,1,0:T(8,128)(2,1)} %constant_dynamic-update-slice_fusion, s32[]{:T(128)S(6)} %select_n.71), kind=kLoop, calls=%fused_computation.76 | loop fusion | bytes 14680068 | tf_op jit(solution)/shard_map/jit(_roll_dynamic)/dynamic_slice | solution.py:20
  144.0 32.9 %while.10 = (s32[]{:T(128)}, f32[2,8,56,12]{2,1,0,3:T(8,128)S(1)}, bf16[2,8,1792,128]{3,2,1,0:T(8,128)(2,1)}, bf16[2,8,12,128,128]{4,3,2,1,0:T(8,128)(2,1)}, s32[]{:T(128)}, /*index=5*/f32[]{:T(128)}) while((s32[]{:T(128)}, f32[2,8,56,12]{2,1,0,3:T(8,128)S(1)}, bf16[2,8,1792,128]{3,2,1,0:T(8,128)(2,1)}, ...), condition=%wide.region_5.6_spmd, body=%wide.region_2.5_spmd.sunk | while | flops 5659164672 | bytes 11065421 | solution.py:66
  144.0 14.4 %convolution_reduce_fusion.2 = f32[8,1792,12]{1,2,0:T(8,128)S(1)} fusion(bf16[2,8,1792,128]{3,2,1,0:T(8,128)(2,1)} %get-tuple-element.89, s32[]{:T(128)} %get-tuple-element.81, bf16[2,8,12,128,128]{4,3,2,1,0:T(8,128)(2,1)} %get-tuple-element.90), kind=kOutput, calls=%fused_computation.3.clone.1 | convolution fusion | flops 5658992640 | bytes 7504896 | tf_op jit(solution)/shard_map/while/body/eval_jaxpr/srd,sgpd->srgp/dot_general | solution.py:24
  158.9 0.8 reshape.220
  160.5 14.4 %convolution_reduce_fusion.2 = f32[8,1792,12]{1,2,0:T(8,128)S(1)} fusion(bf16[2,8,1792,128]{3,2,1,0:T(8,128)(2,1)} %get-tuple-element.89, s32[]{:T(128)} %get-tuple-element.81, bf16[2,8,12,128,128]{4,3,2,1,0:T(8,128)(2,1)} %get-tuple-element.90), kind=kOutput, calls=%fused_computation.3.clone.1 | convolution fusion | flops 5658992640 | bytes 7504896 | tf_op jit(solution)/shard_map/while/body/eval_jaxpr/srd,sgpd->srgp/dot_general | solution.py:24
  175.3 0.8 reshape.220
  177.8 3.5 %all-to-all-start.1 = ((f32[16,1,672]{2,1,0:T(1,128)}), f32[16,1,672]{2,1,0:T(1,128)S(1)}, u32[]{:S(2)}, u32[]{:S(2)}) async-start(f32[16,1,672]{2,1,0:T(1,128)} %reshape.217), calls=%async_computation.1 | async-start | bytes 98304 | tf_op jit(solution)/shard_map/all_to_all | solution.py:70
  181.3 6.7 %all-to-all-done.1 = f32[16,1,672]{2,1,0:T(1,128)S(1)} async-done(((f32[16,1,672]{2,1,0:T(1,128)}), f32[16,1,672]{2,1,0:T(1,128)S(1)}, u32[]{:S(2)}, u32[]{:S(2)}) %all-to-all-start.1) | async-done | bytes 43040 | tf_op jit(solution)/shard_map/all_to_all | solution.py:70
  190.3 3.2 %top_k.9 = (f32[56,128]{1,0:T(8,128)}, s32[56,128]{1,0:T(8,128)}) sort(f32[56,128]{1,0:T(8,128)S(1)} %copy.27, s32[56,128]{1,0:T(8,128)S(1)} %iota.22), dimensions={1}, to_apply=%region_6.7 | sort | flops 93184 | bytes 114688 | tf_op jit(solution)/shard_map/top_k | solution.py:73
  (77 shorter events, 20.3 us)
Async XLA Ops:
  0.6 85.5 %copy-start = (s32[128]{0:T(128)S(1)}, s32[128]{0:T(128)}, u32[]{:S(2)}) copy-start(s32[128]{0:T(128)} %param.8) | copy-start | bytes 1540
  0.6 11.9 %collective-permute-start = (bf16[1,1792,128]{2,1,0:T(8,128)(2,1)}, bf16[1,1792,128]{2,1,0:T(8,128)(2,1)S(1)}, u32[]{:S(2)}, u32[]{:S(2)}) collective-permute-start(bf16[1,1792,128]{2,1,0:T(8,128)(2,1)} %bitcast.79), channel_id=1, source_target_pairs={{0,1},{1,2},{2,3},{3,4},{4,5},{5,6},{6,7},{7,8},{8,9},{9,10},{10,1... | collective-permute-start | bytes 1376264 | tf_op jit(solution)/shard_map/ppermute | solution.py:16
  12.5 10.7 %collective-permute-start.1 = (bf16[1,1792,128]{2,1,0:T(8,128)(2,1)S(1)}, bf16[1,1792,128]{2,1,0:T(8,128)(2,1)S(1)}, u32[]{:S(2)}, u32[]{:S(2)}) collective-permute-start(bf16[1,1792,128]{2,1,0:T(8,128)(2,1)S(1)} %collective-permute-done), channel_id=1, source_target_pairs={{0,1},{1,2},{2,3},{3,4},{4,5},{5,6},{6,7},{7,8},{8,9},{9,10},{10,1... | collective-permute-start | bytes 1376264 | tf_op jit(solution)/shard_map/ppermute | solution.py:16
  12.6 10.8 %collective-permute-start.8 = (bf16[1,1792,128]{2,1,0:T(8,128)(2,1)}, bf16[1,1792,128]{2,1,0:T(8,128)(2,1)S(1)}, u32[]{:S(2)}, u32[]{:S(2)}) collective-permute-start(bf16[1,1792,128]{2,1,0:T(8,128)(2,1)} %bitcast.80), channel_id=1, source_target_pairs={{0,15},{1,0},{2,1},{3,2},{4,3},{5,4},{6,5},{7,6},{8,7},{9,8},{10,9... | collective-permute-start | bytes 1376264 | tf_op jit(solution)/shard_map/ppermute | solution.py:18
  23.3 10.7 %collective-permute-start.2 = (bf16[1,1792,128]{2,1,0:T(8,128)(2,1)S(1)}, bf16[1,1792,128]{2,1,0:T(8,128)(2,1)S(1)}, u32[]{:S(2)}, u32[]{:S(2)}) collective-permute-start(bf16[1,1792,128]{2,1,0:T(8,128)(2,1)S(1)} %collective-permute-done.1), channel_id=1, source_target_pairs={{0,1},{1,2},{2,3},{3,4},{4,5},{5,6},{6,7},{7,8},{8,9},{9,10},{10,1... | collective-permute-start | bytes 1376264 | tf_op jit(solution)/shard_map/ppermute | solution.py:16
  23.3 11.7 %collective-permute-start.9 = (bf16[1,1792,128]{2,1,0:T(8,128)(2,1)S(1)}, bf16[1,1792,128]{2,1,0:T(8,128)(2,1)S(1)}, u32[]{:S(2)}, u32[]{:S(2)}) collective-permute-start(bf16[1,1792,128]{2,1,0:T(8,128)(2,1)S(1)} %collective-permute-done.8), channel_id=1, source_target_pairs={{0,15},{1,0},{2,1},{3,2},{4,3},{5,4},{6,5},{7,6},{8,7},{9,8},{10,9... | collective-permute-start | bytes 1376264 | tf_op jit(solution)/shard_map/ppermute | solution.py:18
  34.0 10.7 %collective-permute-start.3 = (bf16[1,1792,128]{2,1,0:T(8,128)(2,1)S(1)}, bf16[1,1792,128]{2,1,0:T(8,128)(2,1)S(1)}, u32[]{:S(2)}, u32[]{:S(2)}) collective-permute-start(bf16[1,1792,128]{2,1,0:T(8,128)(2,1)S(1)} %collective-permute-done.2), channel_id=1, source_target_pairs={{0,1},{1,2},{2,3},{3,4},{4,5},{5,6},{6,7},{7,8},{8,9},{9,10},{10,1... | collective-permute-start | bytes 1376264 | tf_op jit(solution)/shard_map/ppermute | solution.py:16
  35.0 13.6 %collective-permute-start.10 = (bf16[1,1792,128]{2,1,0:T(8,128)(2,1)S(1)}, bf16[1,1792,128]{2,1,0:T(8,128)(2,1)S(1)}, u32[]{:S(2)}, u32[]{:S(2)}) collective-permute-start(bf16[1,1792,128]{2,1,0:T(8,128)(2,1)S(1)} %collective-permute-done.9), channel_id=1, source_target_pairs={{0,15},{1,0},{2,1},{3,2},{4,3},{5,4},{6,5},{7,6},{8,7},{9,8},{10,9... | collective-permute-start | bytes 1376264 | tf_op jit(solution)/shard_map/ppermute | solution.py:18
  44.7 3.9 %copy-start.2 = (bf16[1,1792,128]{2,1,0:T(8,128)(2,1)}, bf16[1,1792,128]{2,1,0:T(8,128)(2,1)S(1)}, u32[]{:S(2)}) copy-start(bf16[1,1792,128]{2,1,0:T(8,128)(2,1)S(1)} %collective-permute-done.3) | copy-start | bytes 1376260
  44.7 10.7 %collective-permute-start.4 = (bf16[1,1792,128]{2,1,0:T(8,128)(2,1)S(1)}, bf16[1,1792,128]{2,1,0:T(8,128)(2,1)S(1)}, u32[]{:S(2)}, u32[]{:S(2)}) collective-permute-start(bf16[1,1792,128]{2,1,0:T(8,128)(2,1)S(1)} %collective-permute-done.3), channel_id=1, source_target_pairs={{0,1},{1,2},{2,3},{3,4},{4,5},{5,6},{6,7},{7,8},{8,9},{9,10},{10,1... | collective-permute-start | bytes 1376264 | tf_op jit(solution)/shard_map/ppermute | solution.py:16
  48.6 25.4 %collective-permute-start.11 = (bf16[1,1792,128]{2,1,0:T(8,128)(2,1)S(1)}, bf16[1,1792,128]{2,1,0:T(8,128)(2,1)}, u32[]{:S(2)}, u32[]{:S(2)}) collective-permute-start(bf16[1,1792,128]{2,1,0:T(8,128)(2,1)S(1)} %collective-permute-done.10), channel_id=1, source_target_pairs={{0,15},{1,0},{2,1},{3,2},{4,3},{5,4},{6,5},{7,6},{8,7},{9,8},{10,9... | collective-permute-start | bytes 1376264 | tf_op jit(solution)/shard_map/ppermute | solution.py:18
  55.4 19.2 %copy-start.4 = (bf16[1,1792,128]{2,1,0:T(8,128)(2,1)}, bf16[1,1792,128]{2,1,0:T(8,128)(2,1)S(1)}, u32[]{:S(2)}) copy-start(bf16[1,1792,128]{2,1,0:T(8,128)(2,1)S(1)} %collective-permute-done.4) | copy-start | bytes 1376260
  55.4 18.7 %collective-permute-start.5 = (bf16[1,1792,128]{2,1,0:T(8,128)(2,1)S(1)}, bf16[1,1792,128]{2,1,0:T(8,128)(2,1)}, u32[]{:S(2)}, u32[]{:S(2)}) collective-permute-start(bf16[1,1792,128]{2,1,0:T(8,128)(2,1)S(1)} %collective-permute-done.4), channel_id=1, source_target_pairs={{0,1},{1,2},{2,3},{3,4},{4,5},{5,6},{6,7},{7,8},{8,9},{9,10},{10,1... | collective-permute-start | bytes 1376264 | tf_op jit(solution)/shard_map/ppermute | solution.py:16
  60.7 13.2 %all-to-all-start = ((s32[16,1,12]{2,1,0:T(1,128)}), s32[16,1,12]{2,1,0:T(1,128)S(1)}, u32[]{:S(2)}, u32[]{:S(2)}) async-start(s32[16,1,12]{2,1,0:T(1,128)} %bitcast.12), calls=%async_computation | async-start | bytes 16384 | tf_op jit(solution)/shard_map/all_to_all | solution.py:55
  74.0 13.9 %collective-permute-start.12 = (bf16[1,1792,128]{2,1,0:T(8,128)(2,1)}, bf16[1,1792,128]{2,1,0:T(8,128)(2,1)}, u32[]{:S(2)}, u32[]{:S(2)}) collective-permute-start(bf16[1,1792,128]{2,1,0:T(8,128)(2,1)} %collective-permute-done.11), channel_id=1, source_target_pairs={{0,15},{1,0},{2,1},{3,2},{4,3},{5,4},{6,5},{7,6},{8,7},{9,8},{10,9... | collective-permute-start | bytes 1376264 | tf_op jit(solution)/shard_map/ppermute | solution.py:18
  74.1 17.9 %collective-permute-start.6 = (bf16[1,1792,128]{2,1,0:T(8,128)(2,1)}, bf16[1,1792,128]{2,1,0:T(8,128)(2,1)}, u32[]{:S(2)}, u32[]{:S(2)}) collective-permute-start(bf16[1,1792,128]{2,1,0:T(8,128)(2,1)} %collective-permute-done.5), channel_id=1, source_target_pairs={{0,1},{1,2},{2,3},{3,4},{4,5},{5,6},{6,7},{7,8},{8,9},{9,10},{10,1... | collective-permute-start | bytes 1376264 | tf_op jit(solution)/shard_map/ppermute | solution.py:16
  74.6 37.2 %copy-start.1 = (bf16[56,32,128]{2,1,0:T(8,128)(2,1)S(1)}, bf16[56,32,128]{2,1,0:T(8,128)(2,1)}, u32[]{:S(2)}) copy-start(bf16[56,32,128]{2,1,0:T(8,128)(2,1)} %param.6) | copy-start | bytes 1376260
  87.8 19.9 %copy-start.5 = (bf16[1,1792,128]{2,1,0:T(8,128)(2,1)S(1)}, bf16[1,1792,128]{2,1,0:T(8,128)(2,1)}, u32[]{:S(2)}) copy-start(bf16[1,1792,128]{2,1,0:T(8,128)(2,1)} %copy-done.4) | copy-start | bytes 1376260
  87.8 20.7 %copy-start.3 = (bf16[1,1792,128]{2,1,0:T(8,128)(2,1)S(1)}, bf16[1,1792,128]{2,1,0:T(8,128)(2,1)}, u32[]{:S(2)}) copy-start(bf16[1,1792,128]{2,1,0:T(8,128)(2,1)} %copy-done.2) | copy-start | bytes 1376260
  87.9 10.6 %collective-permute-start.13 = (bf16[1,1792,128]{2,1,0:T(8,128)(2,1)}, bf16[1,1792,128]{2,1,0:T(8,128)(2,1)S(1)}, u32[]{:S(2)}, u32[]{:S(2)}) collective-permute-start(bf16[1,1792,128]{2,1,0:T(8,128)(2,1)} %collective-permute-done.12), channel_id=1, source_target_pairs={{0,15},{1,0},{2,1},{3,2},{4,3},{5,4},{6,5},{7,6},{8,7},{9,8},{10,9... | collective-permute-start | bytes 1376264 | tf_op jit(solution)/shard_map/ppermute | solution.py:18
  92.0 11.2 %collective-permute-start.7 = (bf16[1,1792,128]{2,1,0:T(8,128)(2,1)}, bf16[1,1792,128]{2,1,0:T(8,128)(2,1)S(1)}, u32[]{:S(2)}, u32[]{:S(2)}) collective-permute-start(bf16[1,1792,128]{2,1,0:T(8,128)(2,1)} %collective-permute-done.6), channel_id=1, source_target_pairs={{0,1},{1,2},{2,3},{3,4},{4,5},{5,6},{6,7},{7,8},{8,9},{9,10},{10,1... | collective-permute-start | bytes 1376264 | tf_op jit(solution)/shard_map/ppermute | solution.py:16
  98.5 20.9 %collective-permute-start.14 = (bf16[1,1792,128]{2,1,0:T(8,128)(2,1)S(1)}, bf16[1,1792,128]{2,1,0:T(8,128)(2,1)S(1)}, u32[]{:S(2)}, u32[]{:S(2)}) collective-permute-start(bf16[1,1792,128]{2,1,0:T(8,128)(2,1)S(1)} %collective-permute-done.13), channel_id=1, source_target_pairs={{0,15},{1,0},{2,1},{3,2},{4,3},{5,4},{6,5},{7,6},{8,7},{9,8},{10,9... | collective-permute-start | bytes 1376264 | tf_op jit(solution)/shard_map/ppermute | solution.py:18
  144.0 37.3 %copy-start.7 = (s32[1,128]{1,0:T(1,128)S(1)}, s32[1,128]{1,0:T(1,128)}, u32[]{:S(2)}) copy-start(s32[1,128]{1,0:T(1,128)} %param.9) | copy-start | bytes 1540
  177.8 10.2 %all-to-all-start.1 = ((f32[16,1,672]{2,1,0:T(1,128)}), f32[16,1,672]{2,1,0:T(1,128)S(1)}, u32[]{:S(2)}, u32[]{:S(2)}) async-start(f32[16,1,672]{2,1,0:T(1,128)} %reshape.217), calls=%async_computation.1 | async-start | bytes 98304 | tf_op jit(solution)/shard_map/all_to_all | solution.py:70
  190.2 3.2 %copy-start.6 = (f32[56,128]{1,0:T(8,128)}, f32[56,128]{1,0:T(8,128)S(1)}, u32[]{:S(2)}) copy-start(f32[56,128]{1,0:T(8,128)S(1)} %copy.27) | copy-start | bytes 86020
